TPU v7x, 32 devices: a whole 2x2x4 slice. The times are simulated.
32 devices in a mesh: ctx: 8 (over z, x), fsdp: 4 (over y, core).
Axes of the slice: x: 2, y: 2, z: 4, core: 2. Of those that a mesh axis runs over, the one named last changes fastest.
Arguments:
- inputs: bfloat16 [2, 4, 4096, 512], P(None, 'fsdp', 'ctx'), may hold values from -6 to 6
- out_grad: bfloat16 [2, 4, 4096, 512], P(None, 'fsdp', 'ctx'), may hold values from -6 to 6
- segment_ids: int32 [2, 4, 4096], P(None, 'fsdp', 'ctx'), may hold values from 0 to 15, never falling along the last dimension, each value on 1 to 2048 neighbouring positions
- block_order: int32 [16], replicated, may hold values from 0 to 15, each once
- w_qkv: bfloat16 [512, 1536], P('fsdp'), may hold values from -0.25 to 0.25
- w_out: bfloat16 [512, 512], P('fsdp'), may hold values from -1 to 1
- w_up: bfloat16 [512, 2048], P('fsdp'), may hold values from -0.25 to 0.25
- w_down: bfloat16 [2048, 512], P('fsdp'), may hold values from -0.125 to 0.125
- norm1_gain: bfloat16 [512], P('fsdp'), may hold values from 0.25 to 1.75
- norm1_bias: bfloat16 [512], P('fsdp'), may hold values from -2 to 2
- norm2_gain: bfloat16 [512], P('fsdp'), may hold values from 0.25 to 1.75
- norm2_bias: bfloat16 [512], P('fsdp'), may hold values from -2 to 2
- out_bias: bfloat16 [512], P('fsdp'), may hold values from -2 to 2
- up_bias: bfloat16 [2048], P('fsdp'), may hold values from -3 to 3
- down_bias: bfloat16 [512], P('fsdp'), may hold values from -2 to 2
Outputs:
- outputs: bfloat16 [2, 4, 4096, 512], P(None, 'fsdp', 'ctx')
- input_grad: float32 [2, 4, 4096, 512], P(None, 'fsdp', 'ctx')
- grad_w_qkv: float32 [512, 1536], P('fsdp')
- grad_w_out: float32 [512, 512], P('fsdp')
- grad_w_up: float32 [512, 2048], P('fsdp')
- grad_w_down: float32 [2048, 512], P('fsdp')
- grad_norm1_gain: float32 [512], P('fsdp')
- grad_norm1_bias: float32 [512], P('fsdp')
- grad_norm2_gain: float32 [512], P('fsdp')
- grad_norm2_bias: float32 [512], P('fsdp')
- grad_out_bias: float32 [512], P('fsdp')
- grad_up_bias: float32 [2048], P('fsdp')
- grad_down_bias: float32 [512], P('fsdp')
Inputs may be any that keep to these rules, and one draw needn't show every extreme that they name: `segment_ids`: along each sequence's true positions document numbers start at 0 and never fall; each document has 1 to 2048 tokens and one has exactly 2048. `block_order`: each value appears exactly once.
All inputs are finite; a program needn't handle non-finite values.
Results may differ from a plain program's by a relative error of at most 0.02.
Values may be sent and summed in bfloat16 or wider, within the bound.
A program may use at most 256 MiB of HBM per device.

v0:
```python
import math
import jax
import jax.numpy as jnp
from jax import lax
from jax.sharding import PartitionSpec as P

H = 8
HD = 64
BLK = 256
norm_eps = 1e-05
mask_fill = -1e30


def layer_norm(values, gain_vec, offset):
    center = values - jnp.mean(values, axis=-1, keepdims=True)
    spread = jnp.mean(center * center, axis=-1, keepdims=True)
    return center * lax.rsqrt(spread + norm_eps) * gain_vec + offset


def gelu_exact(values):
    return 0.5 * values * (1.0 + lax.erf(values * (1.0 / math.sqrt(2.0))))


def score_block(query_heads, key_heads, query_doc, query_pos, key_doc, key_pos):
    raw_scores = jnp.einsum(
        "qhd,khd->hqk", query_heads, key_heads, preferred_element_type=jnp.float32
    ) * (1.0 / math.sqrt(HD))
    allowed = (query_doc[:, None] == key_doc[None, :]) & (key_pos[None, :] <= query_pos[:, None])
    return (raw_scores, allowed[None])


def soft_block(raw_scores, allowed, log_norm):
    return jnp.exp(jnp.where(allowed, raw_scores, mask_fill) - log_norm[:, :, None])


def row_log_norm(query_heads, key_blocks, doc_blocks, pos_blocks, query_doc, query_pos):

    def row_visit(running, block_item):
        row_top, row_sum = running
        key_heads, key_doc, key_pos = block_item
        raw_scores, allowed = score_block(
            query_heads, key_heads, query_doc, query_pos, key_doc, key_pos
        )
        masked = jnp.where(allowed, raw_scores, mask_fill)
        new_top = jnp.maximum(row_top, jnp.max(masked, axis=-1))
        fresh = jnp.sum(jnp.where(allowed, jnp.exp(masked - new_top[:, :, None]), 0.0), axis=-1)
        return ((new_top, row_sum * jnp.exp(row_top - new_top) + fresh), None)

    query_count = query_doc.shape[0]
    start = (
        jnp.full((H, query_count), mask_fill, jnp.float32),
        jnp.zeros((H, query_count), jnp.float32),
    )
    (row_top, row_sum), unused = lax.scan(row_visit, start, (key_blocks, doc_blocks, pos_blocks))
    return row_top + jnp.log(row_sum)


def attend(
    query_heads, key_blocks, value_blocks, doc_blocks, pos_blocks, query_doc, query_pos, log_norm
):

    def attend_visit(accum_out, block_item):
        key_heads, value_heads, key_doc, key_pos = block_item
        raw_scores, allowed = score_block(
            query_heads, key_heads, query_doc, query_pos, key_doc, key_pos
        )
        soft_low = soft_block(raw_scores, allowed, log_norm).astype(jnp.bfloat16)
        return (
            accum_out
            + jnp.einsum("hqk,khd->qhd", soft_low, value_heads, preferred_element_type=jnp.float32),
            None,
        )

    start = jnp.zeros(query_heads.shape, jnp.float32)
    accum_out, unused = lax.scan(
        attend_visit, start, (key_blocks, value_blocks, doc_blocks, pos_blocks)
    )
    return accum_out


def grad_block(
    query_heads,
    grad_heads,
    log_norm,
    row_delta,
    query_doc,
    query_pos,
    key_heads,
    value_heads,
    key_doc,
    key_pos,
):
    raw_scores, allowed = score_block(
        query_heads, key_heads, query_doc, query_pos, key_doc, key_pos
    )
    soft = soft_block(raw_scores, allowed, log_norm)
    grad_soft = jnp.einsum(
        "qhd,khd->hqk", grad_heads, value_heads, preferred_element_type=jnp.float32
    )
    grad_scores = (soft * (grad_soft - row_delta[:, :, None])).astype(jnp.bfloat16)
    score_scale = 1.0 / math.sqrt(HD)
    part_q = (
        jnp.einsum("hqk,khd->qhd", grad_scores, key_heads, preferred_element_type=jnp.float32)
        * score_scale
    )
    part_k = (
        jnp.einsum("hqk,qhd->khd", grad_scores, query_heads, preferred_element_type=jnp.float32)
        * score_scale
    )
    part_v = jnp.einsum(
        "hqk,qhd->khd", soft.astype(jnp.bfloat16), grad_heads, preferred_element_type=jnp.float32
    )
    return (part_q, part_k, part_v)


def body(
    inputs,
    out_grad,
    segment_ids,
    block_order,
    w_qkv,
    w_out,
    w_up,
    w_down,
    norm1_gain,
    norm1_bias,
    norm2_gain,
    norm2_bias,
    out_bias,
    up_bias,
    down_bias,
):
    gathered = (
        lax.all_gather(w_qkv, "fsdp", axis=0, tiled=True),
        lax.all_gather(w_out, "fsdp", axis=0, tiled=True),
        lax.all_gather(w_up, "fsdp", axis=0, tiled=True),
        lax.all_gather(w_down, "fsdp", axis=0, tiled=True),
        lax.all_gather(norm1_gain, "fsdp", axis=0, tiled=True),
        lax.all_gather(norm1_bias, "fsdp", axis=0, tiled=True),
        lax.all_gather(norm2_gain, "fsdp", axis=0, tiled=True),
        lax.all_gather(norm2_bias, "fsdp", axis=0, tiled=True),
        lax.all_gather(out_bias, "fsdp", axis=0, tiled=True),
        lax.all_gather(up_bias, "fsdp", axis=0, tiled=True),
        lax.all_gather(down_bias, "fsdp", axis=0, tiled=True),
    )
    full_qkv, full_out, full_up, full_down = (gathered[0], gathered[1], gathered[2], gathered[3])
    gain_one, bias_one, gain_two, bias_two, full_obias, full_ubias, full_dbias = [
        member.astype(jnp.float32) for member in gathered[4:]
    ]
    model_width = full_qkv.shape[0]
    local_rows = inputs.shape[2]
    ctx_count = lax.axis_size("ctx")
    seq_len = local_rows * ctx_count
    key_block = min(512, seq_len)
    block_count = seq_len // key_block
    ctx_index = lax.axis_index("ctx")
    row_ids = jnp.arange(local_rows, dtype=jnp.int32)
    own_blocks = lax.dynamic_slice_in_dim(block_order, 2 * ctx_index, 2)
    own_pos = own_blocks[row_ids // BLK] * BLK + row_ids % BLK
    all_ids = jnp.arange(seq_len, dtype=jnp.int32)
    all_pos = block_order[all_ids // BLK] * BLK + all_ids % BLK
    pos_blocks = all_pos.reshape(block_count, key_block)
    grad_sums = [jnp.zeros(member.shape, jnp.float32) for member in gathered]
    outputs_list = []
    input_grads = []
    for micro_idx in range(inputs.shape[0]):
        seq_in = inputs[micro_idx, 0].astype(jnp.float32)
        normed, norm1_pull = jax.vjp(layer_norm, seq_in, gain_one, bias_one)
        normed_low = normed.astype(jnp.bfloat16)
        qkv_out = jnp.dot(normed_low, full_qkv, preferred_element_type=jnp.float32).astype(
            jnp.bfloat16
        )
        query_heads = qkv_out[:, :model_width].reshape(local_rows, H, HD)
        kv_all, doc_all = (
            lax.all_gather(qkv_out[:, model_width:], "ctx", axis=0, tiled=True),
            lax.all_gather(segment_ids[micro_idx, 0], "ctx", axis=0, tiled=True),
        )
        doc_rows = doc_all[all_pos]
        query_doc = doc_all[own_pos]
        kv_heads = kv_all.reshape(block_count, key_block, 2, H, HD)
        key_blocks = kv_heads[:, :, 0]
        value_blocks = kv_heads[:, :, 1]
        doc_blocks = doc_rows.reshape(block_count, key_block)
        log_norm = row_log_norm(query_heads, key_blocks, doc_blocks, pos_blocks, query_doc, own_pos)
        attn_acc = attend(
            query_heads,
            key_blocks,
            value_blocks,
            doc_blocks,
            pos_blocks,
            query_doc,
            own_pos,
            log_norm,
        )
        attn_low = attn_acc.reshape(local_rows, model_width).astype(jnp.bfloat16)
        branch = jnp.dot(attn_low, full_out, preferred_element_type=jnp.float32) + full_obias
        middle = seq_in + branch
        normed_two, norm2_pull = jax.vjp(layer_norm, middle, gain_two, bias_two)
        normed_two_low = normed_two.astype(jnp.bfloat16)
        hidden = jnp.dot(normed_two_low, full_up, preferred_element_type=jnp.float32) + full_ubias
        active, gelu_pull = jax.vjp(gelu_exact, hidden)
        active_low = active.astype(jnp.bfloat16)
        result = middle + (
            jnp.dot(active_low, full_down, preferred_element_type=jnp.float32) + full_dbias
        )
        outputs_list.append(result.astype(jnp.bfloat16))
        grad_y = out_grad[micro_idx, 0]
        grad_y32 = grad_y.astype(jnp.float32)
        grad_sums[3] = grad_sums[3] + jnp.einsum(
            "rf,rd->fd", active_low, grad_y, preferred_element_type=jnp.float32
        )
        grad_sums[10] = grad_sums[10] + jnp.sum(grad_y32, axis=0)
        grad_active = jnp.einsum("rd,fd->rf", grad_y, full_down, preferred_element_type=jnp.float32)
        (grad_hidden,) = gelu_pull(grad_active)
        grad_hidden_low = grad_hidden.astype(jnp.bfloat16)
        grad_sums[2] = grad_sums[2] + jnp.einsum(
            "rd,rf->df", normed_two_low, grad_hidden_low, preferred_element_type=jnp.float32
        )
        grad_sums[9] = grad_sums[9] + jnp.sum(grad_hidden_low.astype(jnp.float32), axis=0)
        grad_normed_two = jnp.einsum(
            "rf,df->rd", grad_hidden_low, full_up, preferred_element_type=jnp.float32
        )
        grad_mid_ln, grad_gain_two, grad_bias_two = norm2_pull(grad_normed_two)
        grad_sums[6] = grad_sums[6] + grad_gain_two
        grad_sums[7] = grad_sums[7] + grad_bias_two
        grad_mid = grad_y32 + grad_mid_ln
        grad_mid_low = grad_mid.astype(jnp.bfloat16)
        grad_sums[1] = grad_sums[1] + jnp.einsum(
            "rd,re->de", attn_low, grad_mid_low, preferred_element_type=jnp.float32
        )
        grad_sums[8] = grad_sums[8] + jnp.sum(grad_mid_low.astype(jnp.float32), axis=0)
        grad_attn_low = jnp.einsum(
            "re,de->rd", grad_mid_low, full_out, preferred_element_type=jnp.float32
        ).astype(jnp.bfloat16)
        grad_heads = grad_attn_low.reshape(local_rows, H, HD)
        row_delta = jnp.sum(grad_heads.astype(jnp.float32) * attn_acc, axis=-1).T

        def back_visit(grad_query, block_item):
            key_heads, value_heads, key_doc, key_pos = block_item
            part_q, part_k, part_v = grad_block(
                query_heads,
                grad_heads,
                log_norm,
                row_delta,
                query_doc,
                own_pos,
                key_heads,
                value_heads,
                key_doc,
                key_pos,
            )
            joined = jnp.concatenate(
                [part_k.reshape(key_block, model_width), part_v.reshape(key_block, model_width)],
                axis=1,
            )
            return (grad_query + part_q, joined)

        grad_query, kv_terms = lax.scan(
            back_visit,
            jnp.zeros((local_rows, H, HD), jnp.float32),
            (key_blocks, value_blocks, doc_blocks, pos_blocks),
        )
        kv_grad = lax.psum_scatter(
            kv_terms.reshape(seq_len, 2 * model_width).astype(jnp.bfloat16),
            "ctx",
            scatter_dimension=0,
            tiled=True,
        ).astype(jnp.float32)
        grad_qkv_low = jnp.concatenate(
            [grad_query.reshape(local_rows, model_width), kv_grad], axis=1
        ).astype(jnp.bfloat16)
        grad_sums[0] = grad_sums[0] + jnp.einsum(
            "rd,re->de", normed_low, grad_qkv_low, preferred_element_type=jnp.float32
        )
        grad_normed = jnp.einsum(
            "re,de->rd", grad_qkv_low, full_qkv, preferred_element_type=jnp.float32
        )
        grad_in_ln, grad_gain_one, grad_bias_one = norm1_pull(grad_normed)
        grad_sums[4] = grad_sums[4] + grad_gain_one
        grad_sums[5] = grad_sums[5] + grad_bias_one
        input_grads.append(grad_mid + grad_in_ln)
    owned = (
        lax.psum_scatter(
            grad_sums[0].astype(jnp.bfloat16), "fsdp", scatter_dimension=0, tiled=True
        ).astype(jnp.float32),
        lax.psum_scatter(
            grad_sums[1].astype(jnp.bfloat16), "fsdp", scatter_dimension=0, tiled=True
        ).astype(jnp.float32),
        lax.psum_scatter(
            grad_sums[2].astype(jnp.bfloat16), "fsdp", scatter_dimension=0, tiled=True
        ).astype(jnp.float32),
        lax.psum_scatter(
            grad_sums[3].astype(jnp.bfloat16), "fsdp", scatter_dimension=0, tiled=True
        ).astype(jnp.float32),
        lax.psum_scatter(
            grad_sums[4].astype(jnp.bfloat16), "fsdp", scatter_dimension=0, tiled=True
        ).astype(jnp.float32),
        lax.psum_scatter(
            grad_sums[5].astype(jnp.bfloat16), "fsdp", scatter_dimension=0, tiled=True
        ).astype(jnp.float32),
        lax.psum_scatter(
            grad_sums[6].astype(jnp.bfloat16), "fsdp", scatter_dimension=0, tiled=True
        ).astype(jnp.float32),
        lax.psum_scatter(
            grad_sums[7].astype(jnp.bfloat16), "fsdp", scatter_dimension=0, tiled=True
        ).astype(jnp.float32),
        lax.psum_scatter(
            grad_sums[8].astype(jnp.bfloat16), "fsdp", scatter_dimension=0, tiled=True
        ).astype(jnp.float32),
        lax.psum_scatter(
            grad_sums[9].astype(jnp.bfloat16), "fsdp", scatter_dimension=0, tiled=True
        ).astype(jnp.float32),
        lax.psum_scatter(
            grad_sums[10].astype(jnp.bfloat16), "fsdp", scatter_dimension=0, tiled=True
        ).astype(jnp.float32),
    )
    summed = (
        lax.psum(owned[0].astype(jnp.bfloat16), "ctx").astype(jnp.float32),
        lax.psum(owned[1].astype(jnp.bfloat16), "ctx").astype(jnp.float32),
        lax.psum(owned[2].astype(jnp.bfloat16), "ctx").astype(jnp.float32),
        lax.psum(owned[3].astype(jnp.bfloat16), "ctx").astype(jnp.float32),
        lax.psum(owned[4].astype(jnp.bfloat16), "ctx").astype(jnp.float32),
        lax.psum(owned[5].astype(jnp.bfloat16), "ctx").astype(jnp.float32),
        lax.psum(owned[6].astype(jnp.bfloat16), "ctx").astype(jnp.float32),
        lax.psum(owned[7].astype(jnp.bfloat16), "ctx").astype(jnp.float32),
        lax.psum(owned[8].astype(jnp.bfloat16), "ctx").astype(jnp.float32),
        lax.psum(owned[9].astype(jnp.bfloat16), "ctx").astype(jnp.float32),
        lax.psum(owned[10].astype(jnp.bfloat16), "ctx").astype(jnp.float32),
    )
    return (
        jnp.stack(outputs_list)[:, None],
        jnp.stack(input_grads)[:, None],
        summed[0],
        summed[1],
        summed[2],
        summed[3],
        summed[4],
        summed[5],
        summed[6],
        summed[7],
        summed[8],
        summed[9],
        summed[10],
    )


def solution(mesh):
    return jax.shard_map(
        body,
        mesh=mesh,
        in_specs=(
            P(None, "fsdp", "ctx", None),
            P(None, "fsdp", "ctx", None),
            P(None, "fsdp", "ctx"),
            P(),
            P("fsdp", None),
            P("fsdp", None),
            P("fsdp", None),
            P("fsdp", None),
            P("fsdp"),
            P("fsdp"),
            P("fsdp"),
            P("fsdp"),
            P("fsdp"),
            P("fsdp"),
            P("fsdp"),
        ),
        out_specs=(
            P(None, "fsdp", "ctx", None),
            P(None, "fsdp", "ctx", None),
            P("fsdp", None),
            P("fsdp", None),
            P("fsdp", None),
            P("fsdp", None),
            P("fsdp"),
            P("fsdp"),
            P("fsdp"),
            P("fsdp"),
            P("fsdp"),
            P("fsdp"),
            P("fsdp"),
        ),
        check_vma=False,
    )
```

profile of v0, /device:TPU:0, one launch (start us, length us, event | category | flops | bytes accessed | tf_op | source)
XLA Modules:
  0.0 1195.3 jit_solution(4293471570105327463)
XLA Ops:
  21.4 10.5 all-gather.15.cloned.1.call-done
  45.4 27.0 %all-gather = s32[1,1,4096]{2,1,0:T(1,128)S(1)} all-gather(s32[1,1,512]{2,1,0:T(1,128)S(1)} %get-tuple-element.1148), channel_id=2, replica_groups=mesh['ctx'=8,'fsdp'=4] {'ctx'}, dimensions={2}, use_global_device_ids=true | all-gather | bytes 18432 | tf_op jit(solution)/shard_map/all_gather | solution.py:176
  85.7 23.0 %gather_fusion.1 = s32[4096]{0:T(1024)S(1)} fusion(s32[4096]{0:T(1024)S(1)} %bitcast.527, s32[4096]{0:T(1024)S(1)} %broadcast_clamp_fusion), kind=kCustom, calls=%fused_computation.1 | custom fusion | bytes 49152 | tf_op jit(solution)/shard_map/gather | solution.py:178
  108.7 26.7 %all-gather.1 = s32[1,1,4096]{2,1,0:T(1,128)S(1)} all-gather(s32[1,1,512]{2,1,0:T(1,128)S(1)} %get-tuple-element.1149), channel_id=3, replica_groups=mesh['ctx'=8,'fsdp'=4] {'ctx'}, dimensions={2}, use_global_device_ids=true | all-gather | bytes 18432 | tf_op jit(solution)/shard_map/all_gather | solution.py:176
  138.6 23.0 %gather_fusion.3 = s32[4096]{0:T(1024)S(1)} fusion(s32[4096]{0:T(1024)S(1)} %bitcast.529, s32[4096]{0:T(1024)S(1)} %broadcast_clamp_fusion), kind=kCustom, calls=%fused_computation.3 | custom fusion | bytes 49152 | tf_op jit(solution)/shard_map/gather | solution.py:178
  182.3 7.2 all_gather.50
  195.1 11.4 copy.162
  206.6 12.2 %copy.239 = bf16[128,8,8,512]{3,2,1,0:T(8,128)(2,1)} copy(bf16[128,8,8,512]{3,1,2,0:T(8,128)(2,1)} %bitcast.538) | data formatting | bytes 16777216
  227.5 50.1 %while.76 = (s32[]{:T(128)}, f32[8,512]{1,0:T(8,128)S(1)}, f32[8,512]{1,0:T(8,128)S(1)}, s32[512]{0:T(512)S(1)}, s32[8,512]{1,0:T(8,128)S(1)}, /*index=5*/s32[8,...) while((s32[]{:T(128)}, f32[8,512]{1,0:T(8,128)S(1)}, ...), condition=%wide.region_15.16_spmd.clone, body=%wide.region_12.15_spmd.clone.sunk | while | flops 286030336 | bytes 18847896 | solution.py:54
  277.6 10.2 all-gather.17.cloned.1.call-done
  287.8 11.7 copy.155
  299.6 12.2 %copy.238 = bf16[128,8,8,512]{3,2,1,0:T(8,128)(2,1)} copy(bf16[128,8,8,512]{3,1,2,0:T(8,128)(2,1)} %bitcast.539) | data formatting | bytes 16777216
  320.5 50.5 %while.74 = (s32[]{:T(128)}, f32[8,512]{1,0:T(8,128)S(1)}, f32[8,512]{1,0:T(8,128)S(1)}, s32[512]{0:T(512)S(1)}, s32[8,512]{1,0:T(8,128)S(1)}, /*index=5*/s32[8,...) while((s32[]{:T(128)}, f32[8,512]{1,0:T(8,128)S(1)}, ...), condition=%wide.region_5.6_spmd.clone, body=%wide.region_2.5_spmd.clone.sunk | while | flops 286030336 | bytes 18847896 | solution.py:54
  377.3 46.4 %while.75 = (s32[]{:T(128)}, f32[512,8,64]{0,2,1:T(8,128)S(1)}, bf16[8,512,8,64]{1,3,2,0:T(8,128)(2,1)}, s32[512]{0:T(512)S(1)}, s32[8,512]{1,0:T(8,128)S(1)}, /...) while((s32[]{:T(128)}, f32[512,8,64]{0,2,1:T(8,128)S(1)}, ...), condition=%wide.region_7.8_spmd.clone, body=%wide.region_6.7_spmd.clone.sunk | while | flops 546580992 | bytes 4234906 | solution.py:75
  430.4 46.4 %while.77 = (s32[]{:T(128)}, f32[512,8,64]{0,2,1:T(8,128)S(1)}, bf16[8,512,8,64]{1,3,2,0:T(8,128)(2,1)}, s32[512]{0:T(512)S(1)}, s32[8,512]{1,0:T(8,128)S(1)}, /...) while((s32[]{:T(128)}, f32[512,8,64]{0,2,1:T(8,128)S(1)}, ...), condition=%wide.region_17.18_spmd.clone, body=%wide.region_16.17_spmd.clone.sunk | while | flops 546580992 | bytes 4234906 | solution.py:75
  525.5 138.9 %while.78 = (s32[]{:T(128)}, f32[512,8,64]{0,2,1:T(8,128)}, bf16[8,512,1024]{2,1,0:T(8,128)(2,1)}, bf16[8,512,8,64]{1,3,2,0:T(8,128)(2,1)}, s32[512]{0:T(512)S(1...) while((s32[]{:T(128)}, f32[512,8,64]{0,2,1:T(8,128)}, ...), condition=%wide.region_24.25_spmd.clone, body=%wide.region_23.24_spmd.clone.sunk | while | flops 1367353856 | bytes 51714240 | solution.py:258
  668.7 131.5 %while.79 = (s32[]{:T(128)}, f32[512,8,64]{0,2,1:T(8,128)}, bf16[8,512,1024]{2,1,0:T(8,128)(2,1)}, bf16[8,512,8,64]{1,3,2,0:T(8,128)(2,1)}, s32[512]{0:T(512)S(1...) while((s32[]{:T(128)}, f32[512,8,64]{0,2,1:T(8,128)}, ...), condition=%wide.region_32.33_spmd.clone, body=%wide.region_31.32_spmd.clone.sunk | while | flops 1367353856 | bytes 51714240 | solution.py:258
  834.8 129.0 %reduce-scatter.9.cloned.1.call-done = bf16[512,1024]{1,0:T(8,128)(2,1)} async-done(((bf16[4096,1024]{1,0:T(8,128)(2,1)}), bf16[512,1024]{1,0:T(8,128)(2,1)}) %reduce-scatter.9.cloned.1.call-update) | async-done | bytes 1048592 | tf_op jit(solution)/shard_map/reduce_scatter | solution.py:263
  987.0 34.2 %reduce-scatter.15.cloned.1.call-done = bf16[128,2048]{1,0:T(8,128)(2,1)} async-done(((bf16[512,2048]{1,0:T(8,128)(2,1)}), bf16[128,2048]{1,0:T(8,128)(2,1)}) %reduce-scatter.15.cloned.1.call-update) | async-done | bytes 524304 | tf_op jit(solution)/shard_map/reduce_scatter | solution.py:289
  1021.1 33.9 %reduce-scatter.17.cloned.1.call-done = bf16[512,512]{1,0:T(8,128)(2,1)} async-done(((bf16[2048,512]{1,0:T(8,128)(2,1)}), bf16[512,512]{1,0:T(8,128)(2,1)}) %reduce-scatter.17.cloned.1.call-update) | async-done | bytes 524304 | tf_op jit(solution)/shard_map/reduce_scatter | solution.py:292
  1055.0 31.5 %reduce-scatter.11.cloned.1.call-done = bf16[128,1536]{1,0:T(8,128)(2,1)} async-done(((bf16[512,1536]{1,0:T(8,128)(2,1)}), bf16[128,1536]{1,0:T(8,128)(2,1)}) %reduce-scatter.11.cloned.1.call-update) | async-done | bytes 393232 | tf_op jit(solution)/shard_map/reduce_scatter | solution.py:283
  1091.7 10.5 all-reduce.9
  1102.8 22.1 %all-reduce.7 = (bf16[128]{0:T(256)(128)(2,1)S(1)}, bf16[128]{0:T(256)(128)(2,1)S(1)}, bf16[128]{0:T(256)(128)(2,1)S(1)}, bf16[128]{0:T(256)(128)(2,1)S(1)}, bf1...) all-reduce(bf16[128]{0:T(256)(128)(2,1)S(1)} %dynamic-slice.1, ...), channel_id=1, replica_groups=mesh['ctx'=8,'fsdp'=4] {'ctx'}, use_global_device_ids=true, to_apply=%region_47.48 | all-reduce | flops 1280 | bytes 5120 | tf_op jit(solution)/shard_map/psum | solution.py:322
  1131.7 48.7 %all-reduce.12.cloned.1.call-done = (bf16[128,1536]{1,0:T(8,128)(2,1)}, bf16[128,512]{1,0:T(8,128)(2,1)}, bf16[128,2048]{1,0:T(8,128)(2,1)}, bf16[512,512]{1,0:T(8,128)(2,1)}) async-done(((bf16[128,1536]{1,0:T(8,128)(2,1)}, bf16[128,512]{1,0:T(8,128)(2,1)}, bf16[128,2048]{1,0:T(8,128)(2,1)}, bf16[512,512]{1,0:T(8,128)(2,1)}), (bf16[128,1536]{1,0:T(8,128)(2,1)}, bf16[128,512]{1,0:T(8,128)(2,1)}, ...) | async-done | bytes 1572880 | tf_op jit(solution)/shard_map/psum | solution.py:318
  (807 shorter events, 689.0 us)
Async XLA Ops:
  7.2 24.8 %all-gather.15.cloned.1.call-start = ((), (), s32[]{:S(2)}) async-start(), calls=%async_computation.6 | async-start | bytes 1966080 | tf_op jit(solution)/shard_map/all_gather | solution.py:134
  7.9 187.2 %all-gather.23.cloned.1.call-start = ((), (), s32[]{:S(2)}) async-start(), calls=%async_computation.10 | async-start | bytes 9437184 | tf_op jit(solution)/shard_map/all_gather | solution.py:175
  36.8 251.0 %all-gather.17.cloned.1.call-start = ((), (), s32[]{:S(2)}) async-start(), calls=%async_computation.7 | async-start | bytes 9437184 | tf_op jit(solution)/shard_map/all_gather | solution.py:175
  37.1 441.5 %copy-start.7 = (bf16[1,1,512,512]{2,3,1,0:T(8,128)(2,1)}, bf16[1,1,512,512]{2,3,1,0:T(8,128)(2,1)S(1)}, u32[]{:S(2)}) copy-start(bf16[1,1,512,512]{2,3,1,0:T(8,128)(2,1)S(1)} %copy.202) | copy-start | bytes 1572868
  40.9 440.4 %all-gather.19.cloned.1.call-start = ((), (), s32[]{:S(2)}) async-start(), calls=%async_computation.8 | async-start | bytes 2621440 | tf_op jit(solution)/shard_map/all_gather | solution.py:136
  41.5 444.9 %all-gather.21.cloned.1.call-start = ((), (), s32[]{:S(2)}) async-start(), calls=%async_computation.9 | async-start | bytes 2621440 | tf_op jit(solution)/shard_map/all_gather | solution.py:137
  42.1 788.4 %reduce-scatter.7.cloned.1.call-start = ((), (), s32[]{:S(2)}) async-start(), calls=%async_computation.11 | async-start | bytes 9437184 | tf_op jit(solution)/shard_map/reduce_scatter | solution.py:263
  138.6 50.9 %copy-start.28 = (bf16[2,1,512,512]{3,2,1,0:T(8,128)(2,1)S(1)}, bf16[2,1,512,512]{3,2,1,0:T(8,128)(2,1)}, u32[]{:S(2)}) copy-start(bf16[2,1,512,512]{3,2,1,0:T(8,128)(2,1)} %param.28) | copy-start | bytes 3145732
  167.0 349.0 %copy-start.47 = (f32[4,1,128]{2,1,0:T(1,128)}, f32[4,1,128]{2,1,0:T(1,128)S(1)}, u32[]{:S(2)}) copy-start(f32[4,1,128]{2,1,0:T(1,128)S(1)} %convert_element_type.307) | copy-start | bytes 6148
  172.0 325.7 %copy-start.53 = (f32[4,1,128]{2,1,0:T(1,128)}, f32[4,1,128]{2,1,0:T(1,128)S(1)}, u32[]{:S(2)}) copy-start(f32[4,1,128]{2,1,0:T(1,128)S(1)} %convert_element_type.308) | copy-start | bytes 6148
  189.5 289.0 %copy-start.9 = (bf16[512,512]{1,0:T(8,128)(2,1)}, bf16[512,512]{1,0:T(8,128)(2,1)S(1)}, u32[]{:S(2)}) copy-start(bf16[512,512]{1,0:T(8,128)(2,1)S(1)} %all_gather.50) | copy-start | bytes 1572868
  664.4 299.4 %reduce-scatter.9.cloned.1.call-start = ((), (), s32[]{:S(2)}) async-start(), calls=%async_computation.12 | async-start | bytes 9437184 | tf_op jit(solution)/shard_map/reduce_scatter | solution.py:263
  800.3 186.7 %reduce-scatter.13.cloned.1.call-start = ((), (), s32[]{:S(2)}) async-start(), calls=%async_computation.14 | async-start | bytes 655360 | tf_op jit(solution)/shard_map/reduce_scatter | solution.py:286
  803.2 218.0 %reduce-scatter.15.cloned.1.call-start = ((), (), s32[]{:S(2)}) async-start(), calls=%async_computation.15 | async-start | bytes 2621440 | tf_op jit(solution)/shard_map/reduce_scatter | solution.py:289
  809.2 245.8 %reduce-scatter.17.cloned.1.call-start = ((), (), s32[]{:S(2)}) async-start(), calls=%async_computation.16 | async-start | bytes 2621440 | tf_op jit(solution)/shard_map/reduce_scatter | solution.py:292
  815.1 271.4 %reduce-scatter.11.cloned.1.call-start = ((), (), s32[]{:S(2)}) async-start(), calls=%async_computation.13 | async-start | bytes 1966080 | tf_op jit(solution)/shard_map/reduce_scatter | solution.py:283
  830.5 133.3 %copy-start.6 = (bf16[1,1,512,512]{2,3,1,0:T(8,128)(2,1)S(1)}, bf16[1,1,512,512]{2,3,1,0:T(8,128)(2,1)}, u32[]{:S(2)}) copy-start(bf16[1,1,512,512]{2,3,1,0:T(8,128)(2,1)} %copy-done.4) | copy-start | bytes 1572868
  830.5 133.3 %copy-start.62 = (f32[512]{0:T(512)S(1)}, f32[512]{0:T(512)}, u32[]{:S(2)}) copy-start(f32[512]{0:T(512)} %copy-done.61) | copy-start | bytes 6148
  830.5 133.3 %copy-start.68 = (f32[512]{0:T(512)S(1)}, f32[512]{0:T(512)}, u32[]{:S(2)}) copy-start(f32[512]{0:T(512)} %copy-done.67) | copy-start | bytes 6148
  968.2 212.2 %all-reduce.12.cloned.1.call-start = ((), (), s32[]{:S(2)}) async-start(), calls=%async_computation.17 | async-start | bytes 3145728 | tf_op jit(solution)/shard_map/psum | solution.py:318
  981.3 105.2 %copy-start.27 = (bf16[1,1,512,512]{2,3,1,0:T(8,128)(2,1)S(1)}, bf16[1,1,512,512]{2,3,1,0:T(8,128)(2,1)}, u32[]{:S(2)}) copy-start(bf16[1,1,512,512]{2,3,1,0:T(8,128)(2,1)} %copy.204) | copy-start | bytes 1572868
  981.3 105.2 %copy-start.78 = (f32[512]{0:T(512)S(1)}, f32[512]{0:T(512)}, u32[]{:S(2)}) copy-start(f32[512]{0:T(512)} %copy-done.77) | copy-start | bytes 6148
  986.3 103.6 %copy-start.23 = (bf16[1,1,512,512]{2,3,1,0:T(8,128)(2,1)S(1)}, bf16[1,1,512,512]{2,3,1,0:T(8,128)(2,1)}, u32[]{:S(2)}) copy-start(bf16[1,1,512,512]{2,3,1,0:T(8,128)(2,1)} %copy.205) | copy-start | bytes 1572868
  986.3 103.6 %copy-start.76 = (f32[512]{0:T(512)S(1)}, f32[512]{0:T(512)}, u32[]{:S(2)}) copy-start(f32[512]{0:T(512)} %copy-done.75) | copy-start | bytes 6148
  (88 other events, 731.3 us)
Sparse Core Ops, SparseCore 0:
  9.6 22.3 all-gather.14
  36.9 125.5 all-gather.22
  164.7 123.0 all-gather.16
  289.2 20.7 all-gather.18
  311.5 22.5 all-gather.20
  664.5 147.1 reduce-scatter.6
  815.8 147.9 reduce-scatter.8
  966.3 20.6 reduce-scatter.12
  989.7 31.4 reduce-scatter.14
  1023.5 31.4 reduce-scatter.16
  1058.3 28.1 reduce-scatter.10
  1090.2 90.2 all-reduce.11
where the time goes:
time: 1210 us; the launch traced here: 1200 us
  matrix products  395 us (33%)
  waiting for transfers between devices  301 us (25%)
  local copies, waits for them, and re-layouts  193 us (16%)
  other arithmetic  155 us (13%)
  blocking collectives  131 us (11%)
  between operations  17.2 us (1%)
    reduce_scatter x2, waiting for transfers between devices, body(): lax.psum_scatter(kv_terms.reshape(seq_len, 2 * model_width).astype(jnp.bf...  129 us
    dot_general x32, matrix products, score_block(): jnp.einsum('qhd,khd->hqk', query_heads, key_heads, preferred_element_type...  77.9 us
    dot_general x16, matrix products, attend_visit(): jnp.einsum('hqk,khd->qhd', soft_low, value_heads, preferred_element_type=...  66.4 us
    dot_general x16, matrix products, grad_block(): jnp.einsum('qhd,khd->hqk', grad_heads, value_heads, preferred_element_typ...  64.5 us
    mul x48, other arithmetic, body(): own_pos = own_blocks[row_ids // BLK] * BLK + row_ids % BLK  62.6 us
    unnamed x219, local copies, waits for them, and re-layouts  55.3 us
    all_gather x2, blocking collectives, body(): lax.all_gather(segment_ids[micro_idx, 0], 'ctx', axis=0, tiled=True)  53.6 us
    dot_general x16, matrix products, grad_block(): jnp.einsum('hqk,khd->qhd', grad_scores, key_heads, preferred_element_type...  50 us
  transfers between devices with their start and end apart: 12, of which 8 were waited for; matrix products, arithmetic and copies ran while one was open for 46% of the time, Pallas kernels for 0%

commit v1 on v0

--- a/solution.py
+++ b/solution.py
@@ -9,6 +9,24 @@
 BLK = 256
 norm_eps = 1e-05
 mask_fill = -1e30
+
+
+def meet_frames(mine_x, ax_name="ctx"):
+    chips = lax.axis_size(ax_name)
+    grid = [(j, (j + 1) % chips) for j in range(chips)]
+    block_list = [(j, (j - 1) % chips) for j in range(chips)]
+    reached, block_next = ([mine_x], [mine_x])
+    for _ in range(chips // 2):
+        reached.append(lax.ppermute(reached[-1], ax_name, grid))
+    num = 0
+    while num < (chips - 1) // 2:
+        block_next.append(lax.ppermute(block_next[-1], axis_name=ax_name, perm=block_list))
+        num = num + 1
+    earlier = jnp.concatenate([*reached[::-1], *block_next[1:]], 0)
+    z_new = jnp.roll(
+        earlier, shift=(lax.axis_index(ax_name) - chips // 2) * mine_x.shape[0], axis=0
+    )
+    return z_new
 
 
 def layer_norm(values, gain_vec, offset):
@@ -172,7 +190,7 @@
         )
         query_heads = qkv_out[:, :model_width].reshape(local_rows, H, HD)
         kv_all, doc_all = (
-            lax.all_gather(qkv_out[:, model_width:], "ctx", axis=0, tiled=True),
+            meet_frames(qkv_out[:, model_width:]),
             lax.all_gather(segment_ids[micro_idx, 0], "ctx", axis=0, tiled=True),
         )
         doc_rows = doc_all[all_pos]

time: 1210 us -> 1530 us (1.26)
  waiting for transfers between devices: 301 us -> 515 us
  blocking collectives: 131 us -> 166 us
  starting transfers between devices: 0.49 us -> 23.7 us
  local copies, waits for them, and re-layouts: 193 us -> 213 us
  other arithmetic: 155 us -> 172 us
    ppermute x0 -> x14, waiting for transfers between devices: none -> 230 us  [the longest x8 188 us: meet_frames(): reached.append(lax.ppermute(reached[-1], ax_name, grid))]
    all_gather x2, blocking collectives: 53.6 us -> 89.3 us  [body(): lax.all_gather(segment_ids[micro_idx, 0], 'ctx', axis=0, tiled=True)]
    all_gather x2 -> x0, local copies, waits for them, and re-layouts: 23.2 us -> none  [body(): lax.all_gather(qkv_out[:, model_width:], 'ctx', axis=0, tiled=True)]
    dynamic_slice x0 -> x2, local copies, waits for them, and re-layouts: none -> 22.6 us  [meet_frames(): jnp.roll(earlier, shift=(lax.axis_index(ax_name) - chips // 2) * mine_x.s...]
    ppermute x0 -> x14, starting transfers between devices: none -> 22.5 us  [the longest x8 13.2 us: meet_frames(): reached.append(lax.ppermute(reached[-1], ax_name, grid))]
    concatenate x0 -> x1, other arithmetic: none -> 17.8 us  [meet_frames(): jnp.roll(earlier, shift=(lax.axis_index(ax_name) - chips // 2) * mine_x.s...]
    unnamed x219 -> x247, local copies, waits for them, and re-layouts: 55.3 us -> 68.4 us
  transfers between devices with their start and end apart: 12 -> 24, of which waited for: 8 -> 13; matrix products, arithmetic and copies ran while one was open for 46% -> 31% of each run, Pallas kernels for 0% -> 0%
where the time goes in v1:
time: 1530 us; the launch traced here: 1510 us
  waiting for transfers between devices  515 us (34%)
  matrix products  403 us (26%)
  local copies, waits for them, and re-layouts  213 us (14%)
  other arithmetic  172 us (11%)
  blocking collectives  166 us (11%)
  starting transfers between devices  23.7 us (2%)
  between operations  17.4 us (1%)
    ppermute x8, waiting for transfers between devices, meet_frames(): reached.append(lax.ppermute(reached[-1], ax_name, grid))  188 us
    reduce_scatter x2, waiting for transfers between devices, body(): lax.psum_scatter(kv_terms.reshape(seq_len, 2 * model_width).astype(jnp.bf...  125 us
    all_gather x2, blocking collectives, body(): lax.all_gather(segment_ids[micro_idx, 0], 'ctx', axis=0, tiled=True)  89.3 us
    dot_general x32, matrix products, score_block(): jnp.einsum('qhd,khd->hqk', query_heads, key_heads, preferred_element_type...  78 us
    dot_general x16, matrix products, attend_visit(): jnp.einsum('hqk,khd->qhd', soft_low, value_heads, preferred_element_type=...  75.7 us
    unnamed x247, local copies, waits for them, and re-layouts  68.4 us
    dot_general x16, matrix products, grad_block(): jnp.einsum('qhd,khd->hqk', grad_heads, value_heads, preferred_element_typ...  64.4 us
    mul x48, other arithmetic, body(): own_pos = own_blocks[row_ids // BLK] * BLK + row_ids % BLK  62.6 us
  transfers between devices with their start and end apart: 24, of which 13 were waited for; matrix products, arithmetic and copies ran while one was open for 31% of the time, Pallas kernels for 0%

profile of v1, /device:TPU:0, one launch (start us, length us, event | category | flops | bytes accessed | tf_op | source)
XLA Modules:
  0.0 1512.1 jit_solution(11973192845284260576)
XLA Ops:
  41.2 22.4 %collective-permute-done = bf16[512,1024]{1,0:T(8,128)(2,1)} collective-permute-done((bf16[512,1024]{1,0:T(8,128)(2,1)S(1)}, bf16[512,1024]{1,0:T(8,128)(2,1)}, u32[]{:S(2)}, u32[]{:S(2)}) %collective-permute-start) | collective-permute-done | bytes 1048608 | tf_op jit(solution)/shard_map/ppermute | solution.py:20
  80.0 47.4 %collective-permute-done.7 = bf16[512,1024]{1,0:T(8,128)(2,1)} collective-permute-done((bf16[512,1024]{1,0:T(8,128)(2,1)}, bf16[512,1024]{1,0:T(8,128)(2,1)}, u32[]{:S(2)}, u32[]{:S(2)}) %collective-permute-start.7) | collective-permute-done | bytes 1048608 | tf_op jit(solution)/shard_map/ppermute | solution.py:20
  129.8 20.0 %collective-permute-done.1 = bf16[512,1024]{1,0:T(8,128)(2,1)} collective-permute-done((bf16[512,1024]{1,0:T(8,128)(2,1)}, bf16[512,1024]{1,0:T(8,128)(2,1)}, u32[]{:S(2)}, u32[]{:S(2)}) %collective-permute-start.1) | collective-permute-done | bytes 1048608 | tf_op jit(solution)/shard_map/ppermute | solution.py:20
  155.9 42.0 %collective-permute-done.4 = bf16[512,1024]{1,0:T(8,128)(2,1)} collective-permute-done((bf16[512,1024]{1,0:T(8,128)(2,1)}, bf16[512,1024]{1,0:T(8,128)(2,1)}, u32[]{:S(2)}, u32[]{:S(2)}) %collective-permute-start.4) | collective-permute-done | bytes 1048608 | tf_op jit(solution)/shard_map/ppermute | solution.py:23
  199.9 39.8 %collective-permute-done.2 = bf16[512,1024]{1,0:T(8,128)(2,1)} collective-permute-done((bf16[512,1024]{1,0:T(8,128)(2,1)}, bf16[512,1024]{1,0:T(8,128)(2,1)}, u32[]{:S(2)}, u32[]{:S(2)}) %collective-permute-start.2) | collective-permute-done | bytes 1048608 | tf_op jit(solution)/shard_map/ppermute | solution.py:20
  243.5 63.3 %all-gather = s32[1,1,4096]{2,1,0:T(1,128)S(1)} all-gather(s32[1,1,512]{2,1,0:T(1,128)S(1)} %get-tuple-element.1149), channel_id=2, replica_groups=mesh['ctx'=8,'fsdp'=4] {'ctx'}, dimensions={2}, use_global_device_ids=true | all-gather | bytes 18432 | tf_op jit(solution)/shard_map/all_gather | solution.py:194
  310.0 23.0 %gather_fusion.1 = s32[4096]{0:T(1024)S(1)} fusion(s32[4096]{0:T(1024)S(1)} %bitcast.527, s32[4096]{0:T(1024)S(1)} %broadcast_clamp_fusion), kind=kCustom, calls=%fused_computation.1 | custom fusion | bytes 49152 | tf_op jit(solution)/shard_map/gather | solution.py:196
  333.0 26.0 %all-gather.1 = s32[1,1,4096]{2,1,0:T(1,128)S(1)} all-gather(s32[1,1,512]{2,1,0:T(1,128)S(1)} %get-tuple-element.1150), channel_id=3, replica_groups=mesh['ctx'=8,'fsdp'=4] {'ctx'}, dimensions={2}, use_global_device_ids=true | all-gather | bytes 18432 | tf_op jit(solution)/shard_map/all_gather | solution.py:194
  362.2 23.0 %gather_fusion.3 = s32[4096]{0:T(1024)S(1)} fusion(s32[4096]{0:T(1024)S(1)} %bitcast.529, s32[4096]{0:T(1024)S(1)} %broadcast_clamp_fusion), kind=kCustom, calls=%fused_computation.3 | custom fusion | bytes 49152 | tf_op jit(solution)/shard_map/gather | solution.py:196
  431.9 57.9 %collective-permute-done.10 = bf16[512,1024]{1,0:T(8,128)(2,1)S(1)} collective-permute-done((bf16[512,1024]{1,0:T(8,128)(2,1)}, bf16[512,1024]{1,0:T(8,128)(2,1)S(1)}, u32[]{:S(2)}, u32[]{:S(2)}) %collective-permute-start.10) | collective-permute-done | bytes 1048608 | tf_op jit(solution)/shard_map/ppermute | solution.py:20
  496.7 17.8 %fusion.144 = (bf16[4096,1024]{1,0:T(8,128)(2,1)}, bf16[4096,1024]{1,0:T(8,128)(2,1)}) fusion(s32[]{:T(128)S(6)} %select_n.277, bf16[4096,1024]{1,0:T(8,128)(2,1)S(1)} %constant_dynamic-update-slice_fusion.10, bf16[4096,1024]{1,0:T(8,128)(2,1)S(1)} %constant_dynamic-update-slice_fusion.2), kind=kLoop, calls=%fused_computation.214 | loop fusion | flops 33554432 | bytes 33554436 | tf_op jit(solution)/shard_map/jit(_roll_dynamic)/concatenate | solution.py:26
  547.0 50.1 %while.76 = (s32[]{:T(128)}, f32[8,512]{1,0:T(8,128)S(1)}, f32[8,512]{1,0:T(8,128)S(1)}, s32[512]{0:T(512)S(1)}, s32[8,512]{1,0:T(8,128)S(1)}, /*index=5*/s32[8,...) while((s32[]{:T(128)}, f32[8,512]{1,0:T(8,128)S(1)}, ...), condition=%wide.region_15.17_spmd.clone, body=%wide.region_12.16_spmd.clone.sunk | while | flops 286030336 | bytes 18847896 | solution.py:72
  602.6 55.3 %while.77 = (s32[]{:T(128)}, f32[512,8,64]{0,2,1:T(8,128)}, bf16[8,512,8,64]{1,3,2,0:T(8,128)(2,1)}, s32[512]{0:T(512)S(1)}, s32[8,512]{1,0:T(8,128)S(1)}, /*ind...) while((s32[]{:T(128)}, f32[512,8,64]{0,2,1:T(8,128)}, ...), condition=%wide.region_17.19_spmd.clone, body=%wide.region_16.18_spmd.clone.sunk | while | flops 546580992 | bytes 4234906 | solution.py:93
  686.9 12.2 copy.234
  707.9 50.3 %while.74 = (s32[]{:T(128)}, f32[8,512]{1,0:T(8,128)S(1)}, f32[8,512]{1,0:T(8,128)S(1)}, s32[512]{0:T(512)S(1)}, s32[8,512]{1,0:T(8,128)S(1)}, /*index=5*/s32[8,...) while((s32[]{:T(128)}, f32[8,512]{1,0:T(8,128)S(1)}, ...), condition=%wide.region_5.7_spmd.clone, body=%wide.region_2.6_spmd.clone.sunk | while | flops 286030336 | bytes 18847896 | solution.py:72
  763.9 46.6 %while.75 = (s32[]{:T(128)}, f32[512,8,64]{0,2,1:T(8,128)S(1)}, bf16[8,512,8,64]{1,3,2,0:T(8,128)(2,1)}, s32[512]{0:T(512)S(1)}, s32[8,512]{1,0:T(8,128)S(1)}, /...) while((s32[]{:T(128)}, f32[512,8,64]{0,2,1:T(8,128)S(1)}, ...), condition=%wide.region_7.9_spmd.clone, body=%wide.region_6.8_spmd.clone.sunk | while | flops 546580992 | bytes 4234906 | solution.py:93
  840.4 138.7 %while.78 = (s32[]{:T(128)}, f32[512,8,64]{0,2,1:T(8,128)}, bf16[8,512,1024]{2,1,0:T(8,128)(2,1)}, bf16[8,512,8,64]{1,3,2,0:T(8,128)(2,1)}, s32[512]{0:T(512)S(1...) while((s32[]{:T(128)}, f32[512,8,64]{0,2,1:T(8,128)}, ...), condition=%wide.region_24.26_spmd.clone, body=%wide.region_23.25_spmd.clone.sunk | while | flops 1367353856 | bytes 51714240 | solution.py:276
  983.9 136.8 %while.79 = (s32[]{:T(128)}, f32[512,8,64]{0,2,1:T(8,128)}, bf16[8,512,1024]{2,1,0:T(8,128)(2,1)}, bf16[8,512,8,64]{1,3,2,0:T(8,128)(2,1)}, s32[512]{0:T(512)S(1...) while((s32[]{:T(128)}, f32[512,8,64]{0,2,1:T(8,128)}, ...), condition=%wide.region_32.34_spmd.clone, body=%wide.region_31.33_spmd.clone.sunk | while | flops 1367353856 | bytes 51714240 | solution.py:276
  1155.3 125.2 %reduce-scatter.9.cloned.1.call-done = bf16[512,1024]{1,0:T(8,128)(2,1)} async-done(((bf16[4096,1024]{1,0:T(8,128)(2,1)}), bf16[512,1024]{1,0:T(8,128)(2,1)}) %reduce-scatter.9.cloned.1.call-update) | async-done | bytes 1048592 | tf_op jit(solution)/shard_map/reduce_scatter | solution.py:281
  1303.5 34.2 %reduce-scatter.15.cloned.1.call-done = bf16[128,2048]{1,0:T(8,128)(2,1)} async-done(((bf16[512,2048]{1,0:T(8,128)(2,1)}), bf16[128,2048]{1,0:T(8,128)(2,1)}) %reduce-scatter.15.cloned.1.call-update) | async-done | bytes 524304 | tf_op jit(solution)/shard_map/reduce_scatter | solution.py:307
  1337.7 34.0 %reduce-scatter.17.cloned.1.call-done = bf16[512,512]{1,0:T(8,128)(2,1)} async-done(((bf16[2048,512]{1,0:T(8,128)(2,1)}), bf16[512,512]{1,0:T(8,128)(2,1)}) %reduce-scatter.17.cloned.1.call-update) | async-done | bytes 524304 | tf_op jit(solution)/shard_map/reduce_scatter | solution.py:310
  1371.7 31.5 %reduce-scatter.11.cloned.1.call-done = bf16[128,1536]{1,0:T(8,128)(2,1)} async-done(((bf16[512,1536]{1,0:T(8,128)(2,1)}), bf16[128,1536]{1,0:T(8,128)(2,1)}) %reduce-scatter.11.cloned.1.call-update) | async-done | bytes 393232 | tf_op jit(solution)/shard_map/reduce_scatter | solution.py:301
  1419.5 22.0 %all-reduce.7 = (bf16[128]{0:T(256)(128)(2,1)S(1)}, bf16[128]{0:T(256)(128)(2,1)S(1)}, bf16[128]{0:T(256)(128)(2,1)S(1)}, bf16[128]{0:T(256)(128)(2,1)S(1)}, bf1...) all-reduce(bf16[128]{0:T(256)(128)(2,1)S(1)} %dynamic-slice.1, ...), channel_id=1, replica_groups=mesh['ctx'=8,'fsdp'=4] {'ctx'}, use_global_device_ids=true, to_apply=%region_47.49 | all-reduce | flops 1280 | bytes 5120 | tf_op jit(solution)/shard_map/psum | solution.py:340
  1448.4 48.8 %all-reduce.12.cloned.1.call-done = (bf16[128,1536]{1,0:T(8,128)(2,1)}, bf16[128,512]{1,0:T(8,128)(2,1)}, bf16[128,2048]{1,0:T(8,128)(2,1)}, bf16[512,512]{1,0:T(8,128)(2,1)}) async-done(((bf16[128,1536]{1,0:T(8,128)(2,1)}, bf16[128,512]{1,0:T(8,128)(2,1)}, bf16[128,2048]{1,0:T(8,128)(2,1)}, bf16[512,512]{1,0:T(8,128)(2,1)}), (bf16[128,1536]{1,0:T(8,128)(2,1)}, bf16[128,512]{1,0:T(8,128)(2,1)}, ...) | async-done | bytes 1572880 | tf_op jit(solution)/shard_map/psum | solution.py:336
  (860 shorter events, 801.2 us)
Async XLA Ops:
  7.2 24.8 %all-gather.13.cloned.1.call-start = ((), (), s32[]{:S(2)}) async-start(), calls=%async_computation.6 | async-start | bytes 1966080 | tf_op jit(solution)/shard_map/all_gather | solution.py:152
  7.9 652.6 %all-gather.15.cloned.1.call-start = ((), (), s32[]{:S(2)}) async-start(), calls=%async_computation.7 | async-start | bytes 2621440 | tf_op jit(solution)/shard_map/all_gather | solution.py:154
  8.7 657.4 %all-gather.17.cloned.1.call-start = ((), (), s32[]{:S(2)}) async-start(), calls=%async_computation.8 | async-start | bytes 2621440 | tf_op jit(solution)/shard_map/all_gather | solution.py:155
  34.8 28.8 %collective-permute-start = (bf16[512,1024]{1,0:T(8,128)(2,1)S(1)}, bf16[512,1024]{1,0:T(8,128)(2,1)}, u32[]{:S(2)}, u32[]{:S(2)}) collective-permute-start(bf16[512,1024]{1,0:T(8,128)(2,1)S(1)} %slice.84), channel_id=1, source_target_pairs={{0,4},{4,8},{8,12},{12,16},{16,20},{20,24},{24,28},{28,0},{1,5},{5... | collective-permute-start | bytes 3145736 | tf_op jit(solution)/shard_map/ppermute | solution.py:20
  39.7 87.6 %collective-permute-start.7 = (bf16[512,1024]{1,0:T(8,128)(2,1)}, bf16[512,1024]{1,0:T(8,128)(2,1)}, u32[]{:S(2)}, u32[]{:S(2)}) collective-permute-start(bf16[512,1024]{1,0:T(8,128)(2,1)} %slice.88), channel_id=1, source_target_pairs={{0,4},{4,8},{8,12},{12,16},{16,20},{20,24},{24,28},{28,0},{1,5},{5... | collective-permute-start | bytes 3145736 | tf_op jit(solution)/shard_map/ppermute | solution.py:20
  63.7 86.2 %collective-permute-start.1 = (bf16[512,1024]{1,0:T(8,128)(2,1)}, bf16[512,1024]{1,0:T(8,128)(2,1)}, u32[]{:S(2)}, u32[]{:S(2)}) collective-permute-start(bf16[512,1024]{1,0:T(8,128)(2,1)} %collective-permute-done), channel_id=1, source_target_pairs={{0,4},{4,8},{8,12},{12,16},{16,20},{20,24},{24,28},{28,0},{1,5},{5... | collective-permute-start | bytes 3145736 | tf_op jit(solution)/shard_map/ppermute | solution.py:20
  63.7 1087.4 %reduce-scatter.7.cloned.1.call-start = ((), (), s32[]{:S(2)}) async-start(), calls=%async_computation.9 | async-start | bytes 9437184 | tf_op jit(solution)/shard_map/reduce_scatter | solution.py:281
  75.2 77.9 %collective-permute-start.11 = (bf16[512,1024]{1,0:T(8,128)(2,1)}, bf16[512,1024]{1,0:T(8,128)(2,1)}, u32[]{:S(2)}, u32[]{:S(2)}) collective-permute-start(bf16[512,1024]{1,0:T(8,128)(2,1)} %slice.88), channel_id=1, source_target_pairs={{0,28},{4,0},{8,4},{12,8},{16,12},{20,16},{24,20},{28,24},{1,29},{... | collective-permute-start | bytes 3145736 | tf_op jit(solution)/shard_map/ppermute | solution.py:23
  79.9 118.0 %collective-permute-start.4 = (bf16[512,1024]{1,0:T(8,128)(2,1)}, bf16[512,1024]{1,0:T(8,128)(2,1)}, u32[]{:S(2)}, u32[]{:S(2)}) collective-permute-start(bf16[512,1024]{1,0:T(8,128)(2,1)} %copy-done.47), channel_id=1, source_target_pairs={{0,28},{4,0},{8,4},{12,8},{16,12},{20,16},{24,20},{28,24},{1,29},{... | collective-permute-start | bytes 3145736 | tf_op jit(solution)/shard_map/ppermute | solution.py:23
  127.4 71.0 %collective-permute-start.8 = (bf16[512,1024]{1,0:T(8,128)(2,1)}, bf16[512,1024]{1,0:T(8,128)(2,1)}, u32[]{:S(2)}, u32[]{:S(2)}) collective-permute-start(bf16[512,1024]{1,0:T(8,128)(2,1)} %collective-permute-done.7), channel_id=1, source_target_pairs={{0,4},{4,8},{8,12},{12,16},{16,20},{20,24},{24,28},{28,0},{1,5},{5... | collective-permute-start | bytes 3145736 | tf_op jit(solution)/shard_map/ppermute | solution.py:20
  149.8 89.9 %collective-permute-start.2 = (bf16[512,1024]{1,0:T(8,128)(2,1)}, bf16[512,1024]{1,0:T(8,128)(2,1)}, u32[]{:S(2)}, u32[]{:S(2)}) collective-permute-start(bf16[512,1024]{1,0:T(8,128)(2,1)} %collective-permute-done.1), channel_id=1, source_target_pairs={{0,4},{4,8},{8,12},{12,16},{16,20},{20,24},{24,28},{28,0},{1,5},{5... | collective-permute-start | bytes 3145736 | tf_op jit(solution)/shard_map/ppermute | solution.py:20
  153.0 268.6 %collective-permute-start.12 = (bf16[512,1024]{1,0:T(8,128)(2,1)}, bf16[512,1024]{1,0:T(8,128)(2,1)}, u32[]{:S(2)}, u32[]{:S(2)}) collective-permute-start(bf16[512,1024]{1,0:T(8,128)(2,1)} %collective-permute-done.11), channel_id=1, source_target_pairs={{0,28},{4,0},{8,4},{12,8},{16,12},{20,16},{24,20},{28,24},{1,29},{... | collective-permute-start | bytes 3145736 | tf_op jit(solution)/shard_map/ppermute | solution.py:23
  197.9 223.8 %collective-permute-start.5 = (bf16[512,1024]{1,0:T(8,128)(2,1)}, bf16[512,1024]{1,0:T(8,128)(2,1)}, u32[]{:S(2)}, u32[]{:S(2)}) collective-permute-start(bf16[512,1024]{1,0:T(8,128)(2,1)} %collective-permute-done.4), channel_id=1, source_target_pairs={{0,28},{4,0},{8,4},{12,8},{16,12},{20,16},{24,20},{28,24},{1,29},{... | collective-permute-start | bytes 3145736 | tf_op jit(solution)/shard_map/ppermute | solution.py:23
  198.4 224.3 %collective-permute-start.9 = (bf16[512,1024]{1,0:T(8,128)(2,1)}, bf16[512,1024]{1,0:T(8,128)(2,1)}, u32[]{:S(2)}, u32[]{:S(2)}) collective-permute-start(bf16[512,1024]{1,0:T(8,128)(2,1)} %collective-permute-done.8), channel_id=1, source_target_pairs={{0,4},{4,8},{8,12},{12,16},{16,20},{20,24},{24,28},{28,0},{1,5},{5... | collective-permute-start | bytes 3145736 | tf_op jit(solution)/shard_map/ppermute | solution.py:20
  239.7 184.2 %collective-permute-start.3 = (bf16[512,1024]{1,0:T(8,128)(2,1)}, bf16[512,1024]{1,0:T(8,128)(2,1)}, u32[]{:S(2)}, u32[]{:S(2)}) collective-permute-start(bf16[512,1024]{1,0:T(8,128)(2,1)} %collective-permute-done.2), channel_id=1, source_target_pairs={{0,4},{4,8},{8,12},{12,16},{16,20},{20,24},{24,28},{28,0},{1,5},{5... | collective-permute-start | bytes 3145736 | tf_op jit(solution)/shard_map/ppermute | solution.py:20
  421.6 75.0 %collective-permute-start.13 = (bf16[512,1024]{1,0:T(8,128)(2,1)}, bf16[512,1024]{1,0:T(8,128)(2,1)S(1)}, u32[]{:S(2)}, u32[]{:S(2)}) collective-permute-start(bf16[512,1024]{1,0:T(8,128)(2,1)} %collective-permute-done.12), channel_id=1, source_target_pairs={{0,28},{4,0},{8,4},{12,8},{16,12},{20,16},{24,20},{28,24},{1,29},{... | collective-permute-start | bytes 3145736 | tf_op jit(solution)/shard_map/ppermute | solution.py:23
  421.7 74.8 %collective-permute-start.6 = (bf16[512,1024]{1,0:T(8,128)(2,1)}, bf16[512,1024]{1,0:T(8,128)(2,1)S(1)}, u32[]{:S(2)}, u32[]{:S(2)}) collective-permute-start(bf16[512,1024]{1,0:T(8,128)(2,1)} %collective-permute-done.5), channel_id=1, source_target_pairs={{0,28},{4,0},{8,4},{12,8},{16,12},{20,16},{24,20},{28,24},{1,29},{... | collective-permute-start | bytes 3145736 | tf_op jit(solution)/shard_map/ppermute | solution.py:23
  422.7 67.1 %collective-permute-start.10 = (bf16[512,1024]{1,0:T(8,128)(2,1)}, bf16[512,1024]{1,0:T(8,128)(2,1)S(1)}, u32[]{:S(2)}, u32[]{:S(2)}) collective-permute-start(bf16[512,1024]{1,0:T(8,128)(2,1)} %collective-permute-done.9), channel_id=1, source_target_pairs={{0,4},{4,8},{8,12},{12,16},{16,20},{20,24},{24,28},{28,0},{1,5},{5... | collective-permute-start | bytes 3145736 | tf_op jit(solution)/shard_map/ppermute | solution.py:20
  979.1 301.4 %reduce-scatter.9.cloned.1.call-start = ((), (), s32[]{:S(2)}) async-start(), calls=%async_computation.10 | async-start | bytes 9437184 | tf_op jit(solution)/shard_map/reduce_scatter | solution.py:281
  1120.8 182.7 %reduce-scatter.13.cloned.1.call-start = ((), (), s32[]{:S(2)}) async-start(), calls=%async_computation.12 | async-start | bytes 655360 | tf_op jit(solution)/shard_map/reduce_scatter | solution.py:304
  1123.7 213.9 %reduce-scatter.15.cloned.1.call-start = ((), (), s32[]{:S(2)}) async-start(), calls=%async_computation.13 | async-start | bytes 2621440 | tf_op jit(solution)/shard_map/reduce_scatter | solution.py:307
  1129.7 241.9 %reduce-scatter.17.cloned.1.call-start = ((), (), s32[]{:S(2)}) async-start(), calls=%async_computation.14 | async-start | bytes 2621440 | tf_op jit(solution)/shard_map/reduce_scatter | solution.py:310
  1135.9 267.3 %reduce-scatter.11.cloned.1.call-start = ((), (), s32[]{:S(2)}) async-start(), calls=%async_computation.11 | async-start | bytes 1966080 | tf_op jit(solution)/shard_map/reduce_scatter | solution.py:301
  1284.9 212.2 %all-reduce.12.cloned.1.call-start = ((), (), s32[]{:S(2)}) async-start(), calls=%async_computation.15 | async-start | bytes 3145728 | tf_op jit(solution)/shard_map/psum | solution.py:336
  (106 other events, 4223.2 us)
Sparse Core Ops, SparseCore 0:
  9.6 22.3 all-gather.12
  33.5 22.5 all-gather.14
  63.8 23.0 all-gather.16
  979.2 149.3 reduce-scatter.6
  1132.5 147.9 reduce-scatter.8
  1282.8 20.6 reduce-scatter.12
  1306.2 31.4 reduce-scatter.14
  1340.2 31.4 reduce-scatter.16
  1375.0 28.1 reduce-scatter.10
  1406.8 90.2 all-reduce.11
